TPU v7x, 32 devices: a whole 2x2x4 slice. The times are simulated.
32 devices in a mesh: blk: 8 (over z, y), head: 4 (over x, core).
Axes of the slice: x: 2, y: 2, z: 4, core: 2. Of those that a mesh axis runs over, the one named last changes fastest.
Arguments:
- queries: bfloat16 [4096, 1024], P('blk', 'head'), may hold values from -170 to 170
- key_rows: bfloat16 [4096, 1024], P('blk', 'head'), may hold values from -9 to 9
- values: bfloat16 [4096, 1024], P('blk', 'head'), may hold values from -48 to 48
- text_keys: bfloat16 [308, 1024], P(None, 'head'), may hold values from -9 to 9
- text_values: bfloat16 [308, 1024], P(None, 'head'), may hold values from -48 to 48
- block_image: int32 [32], replicated, may hold values from 0 to 1, as said below
- gate_image: float32 [2, 1536], replicated, may hold values from 0.5 to 2
- residual: bfloat16 [4096, 1536], P(('blk', 'head')), may hold values from -6 to 6
- w_out: bfloat16 [1024, 1536], P('head'), may hold values from -0.1875 to 0.1875
Outputs:
- stream_out: bfloat16 [4096, 1536], P(('blk', 'head'))
Inputs may be any that keep to these rules, and one draw needn't show every extreme that they name: `block_image`: each image number 0 to 1 names 8 to 24 of the entries, some image exactly 24 and some exactly 8; the blocks of an image lie anywhere in the array.
All inputs are finite; a program needn't handle non-finite values.
Results may differ from a plain program's by a relative error of at most 0.014.
Values may be sent and summed in bfloat16 or wider, within the bound.
No kernel may reach another device: no remote copies, remote signals or barrier semaphores. Data moves between devices by JAX's collectives and lax.ppermute only.
A program may use at most 64 MiB of HBM per device.

v0:
```python
import math

import jax
import jax.numpy as jnp
from jax import lax
from jax.experimental import pallas as pl
from jax.experimental.pallas import tpu as pltpu
from jax.sharding import PartitionSpec as P

HD = 64
TEXT = 154
BS = 128
GROUP = 2
WIDE = 8


neg_large = -1e30


def absorb(running, query_three, query_image, key_slab, value_slab, key_image):
    best, total, accum = running
    heads = query_three.shape[1]
    width = query_three.shape[2]
    key_three = key_slab.reshape(key_slab.shape[0], heads, width)
    value_three = value_slab.reshape(value_slab.shape[0], heads, width)
    scores = jnp.einsum("qhd,khd->hqk", query_three, key_three, preferred_element_type=jnp.float32)
    scores = scores * (1.0 / math.sqrt(width))
    allowed = query_image[:, None] == key_image[None, :]
    scores = jnp.where(allowed[None], scores, neg_large)
    newbest = jnp.maximum(best, jnp.max(scores, axis=2))
    weights = jnp.exp(scores - newbest[..., None])
    shrink = jnp.exp(best - newbest)
    total = total * shrink + jnp.sum(weights, axis=2)
    update = jnp.einsum(
        "hqk,khd->hqd",
        weights.astype(jnp.bfloat16),
        value_three,
        preferred_element_type=jnp.float32,
    )
    accum = accum * shrink[..., None] + update
    return (newbest, total, accum)


def on_device(
    queries, key_rows, values, text_keys, text_values, block_image, gate_image, residual, w_out
):
    tok_blk = queries.shape[0]
    ncols = queries.shape[1]
    heads_here = ncols // HD
    blocks_here = tok_blk // BS
    token_image = jnp.repeat(block_image, BS)
    blk_index = lax.axis_index("blk")
    my_blocks = lax.dynamic_slice_in_dim(block_image, blk_index * blocks_here, blocks_here)
    query_image = jnp.repeat(my_blocks, BS)
    text_image = jnp.arange(text_keys.shape[0]) // TEXT
    start_state = (
        jnp.full((heads_here, tok_blk), neg_large, jnp.float32),
        jnp.zeros((heads_here, tok_blk), jnp.float32),
        jnp.zeros((heads_here, tok_blk, HD), jnp.float32),
    )
    query_three = queries.reshape(tok_blk, heads_here, HD)
    running = absorb(start_state, query_three, query_image, text_keys, text_values, text_image)
    fold_running = running
    key_piece = lax.all_gather(key_rows, "blk", axis=0, tiled=True)
    value_piece = lax.all_gather(values, "blk", axis=0, tiled=True)
    length = key_piece.shape[0]

    def advance(state, position):
        begin = position * tok_blk
        key_slab = lax.dynamic_slice_in_dim(key_piece, begin, tok_blk)
        value_slab = lax.dynamic_slice_in_dim(value_piece, begin, tok_blk)
        slab_image = lax.dynamic_slice_in_dim(token_image, begin, tok_blk)
        return (absorb(state, query_three, query_image, key_slab, value_slab, slab_image), None)

    fold_running, unused = lax.scan(
        advance, fold_running, jnp.arange(length // tok_blk, dtype=jnp.int32)
    )
    best, total, accum = fold_running
    attended = (accum / total[..., None]).astype(jnp.bfloat16)
    attended = attended.transpose(1, 0, 2).reshape(tok_blk, ncols)
    tok_dev = tok_blk // lax.axis_size("head")
    mixed = lax.all_to_all(attended, "head", split_axis=0, concat_axis=1, tiled=True)
    projected = jnp.dot(
        mixed, lax.all_gather(w_out, "head", axis=0, tiled=True), preferred_element_type=jnp.float32
    )
    head_index = lax.axis_index("head")
    row_image = lax.dynamic_slice_in_dim(query_image, head_index * tok_dev, tok_dev)
    onehot = (
        row_image[:, None] == jnp.arange(gate_image.shape[0], dtype=jnp.int32)[None, :]
    ).astype(jnp.float32)
    gating = jnp.dot(onehot, gate_image, precision=lax.Precision.HIGHEST)
    return (residual.astype(jnp.float32) + gating * projected).astype(jnp.bfloat16)

def round_up(count, unit):
    return -(-count // unit) * unit


def pack_kernel(head_ref, q_ref, k_ref, v_ref, tk_ref, tv_ref, send_ref, text_ref):
    heads = q_ref.shape[1] // HD
    rows = q_ref.shape[0]
    half = rows // 2
    for h in range(heads):
        cols = slice(h * HD, (h + 1) * HD)
        send_ref[h, 0:rows, :] = jnp.concatenate([k_ref[:, cols], v_ref[:, cols]], axis=1)
        send_ref[h, rows : rows + half, :] = jnp.concatenate(
            [q_ref[0:half, cols], q_ref[half:rows, cols]], axis=1
        )
    ntext = tk_ref.shape[0]
    text_ref[...] = jnp.zeros(text_ref.shape, text_ref.dtype)
    for h in range(heads):

        @pl.when(head_ref[0] == h)
        def _():
            cols = slice(h * HD, (h + 1) * HD)
            text_ref[0:ntext, :] = jnp.concatenate([tk_ref[:, cols], tv_ref[:, cols]], axis=1)


EXPONENT = math.log2(math.e) / math.sqrt(HD)


def count_images(image_ref, count_ref, which, parts, sources, per):
    def tally(s, carry):
        for i in range(per):
            image = image_ref[(s * parts + which) * per + i]
            count_ref[image] = count_ref[image] + 1
        return carry

    for i in range(count_ref.shape[0]):
        count_ref[i] = 0
    lax.fori_loop(0, sources, tally, 0)


def put_block(keys_ref, vals_ref, spot, block):
    at = pl.ds(pl.multiple_of(spot * BS, BS), BS)
    lane = lax.broadcasted_iota(jnp.int32, block.shape, 1)
    keys_ref[at, :] = block
    vals_ref[at, :] = jnp.where(lane < HD, jnp.ones_like(block), block)


def score(query, slab):
    return lax.dot_general(query, slab, (((1,), (1,)), ((), ())), preferred_element_type=jnp.float32)


def fold(state, scores, vals):
    best, accum = state
    newbest = jnp.maximum(best, jnp.max(scores, axis=1, keepdims=True))
    weights = jnp.exp2((scores - newbest) * EXPONENT).astype(jnp.bfloat16)
    shrink = jnp.exp2((best - newbest) * EXPONENT)
    update = jnp.dot(weights, vals, preferred_element_type=jnp.float32)
    return (newbest, accum * shrink + update)


def first_kernel(
    image_ref, where_ref, got_ref, text_ref, q_ref, best_ref, accum_ref,
    keys_ref, vals_ref, count_ref, start_ref, qstart_ref
):
    images = count_ref.shape[0]
    sources = got_ref.shape[0]
    rows = got_ref.shape[1] * 2 // 3
    per = rows // BS
    parts = image_ref.shape[0] // (sources * per)
    mine = where_ref[0]
    count_images(image_ref, count_ref, mine, parts, sources, per)
    begin = jnp.int32(0)
    qbegin = jnp.int32(0)
    for i in range(images):
        start_ref[i] = begin
        qstart_ref[i] = qbegin
        begin = begin + count_ref[i]
        qbegin = qbegin + (count_ref[i] + GROUP - 1) // GROUP * GROUP
    q_ref[...] = jnp.zeros(q_ref.shape, q_ref.dtype)

    def place(s, carry):
        for i in range(per):
            image = image_ref[(s * parts + mine) * per + i]
            spot = start_ref[image]
            start_ref[image] = spot + 1
            put_block(keys_ref, vals_ref, spot, got_ref[s, i * BS : (i + 1) * BS, :])
            half = per // 2
            qrow = rows + (i % half) * BS
            part = got_ref[s, qrow : qrow + BS, :]
            if i >= half:
                part = jnp.concatenate([part[:, HD:], part[:, :HD]], axis=1)
            lane = lax.broadcasted_iota(jnp.int32, part.shape, 1)
            qspot = qstart_ref[image]
            qstart_ref[image] = qspot + 1
            q_ref[pl.ds(pl.multiple_of(qspot * BS, BS), BS), :] = jnp.where(
                lane < HD, part, jnp.zeros_like(part)
            )
        return carry

    lax.fori_loop(0, sources, place, 0)

    def one_image(image, carry):
        count = count_ref[image]
        first = start_ref[image] - count
        qfirst = qstart_ref[image] - count
        text_at = image * TEXT
        shift = text_at % 16
        window = text_ref[pl.ds(pl.multiple_of(text_at - shift, 16), 256), :]
        lane = lax.broadcasted_iota(jnp.int32, window.shape, 1)
        text_vals = jnp.where(lane < HD, jnp.ones_like(window), window)
        spot = lax.broadcasted_iota(jnp.int32, (1, 256), 1)
        text_ok = (spot >= shift) & (spot < shift + TEXT)

        def one_tile(t, carry):
            at = pl.ds(pl.multiple_of((qfirst + t * GROUP) * BS, BS), GROUP * BS)
            query = q_ref[at, :]
            scores = jnp.where(text_ok, score(query, window), neg_large)
            best = jnp.max(scores, axis=1, keepdims=True)
            weights = jnp.exp2((scores - best) * EXPONENT).astype(jnp.bfloat16)
            accum = jnp.dot(weights, text_vals, preferred_element_type=jnp.float32)

            def full(c, state):
                row = pl.ds(pl.multiple_of((first + c * WIDE) * BS, BS), WIDE * BS)
                return fold(state, score(query, keys_ref[row, :]), vals_ref[row, :])

            best, accum = lax.fori_loop(0, count // WIDE, full, (best, accum))
            best_ref[at, :] = jnp.broadcast_to(best, accum.shape)
            accum_ref[at, :] = accum
            return carry

        return lax.fori_loop(0, (count + GROUP - 1) // GROUP, one_tile, carry)

    lax.fori_loop(0, images, one_image, 0)


def second_kernel(
    image_ref, where_ref, got_ref, far_ref, q_ref, best_ref, accum_ref, out_ref,
    keys_ref, vals_ref, o_ref, count_ref, start_ref, qstart_ref, far_count_ref, seen_ref, pos_ref
):
    images = count_ref.shape[0]
    sources, rows = far_ref.shape[0], far_ref.shape[1]
    per = rows // BS
    parts = image_ref.shape[0] // (sources * per)
    mine = where_ref[0]
    other = 1 - mine
    count_images(image_ref, count_ref, mine, parts, sources, per)
    count_images(image_ref, far_count_ref, other, parts, sources, per)
    begin = jnp.int32(0)
    qbegin = jnp.int32(0)
    for i in range(images):
        far_count_ref[i] = far_count_ref[i] + count_ref[i] % WIDE
        seen_ref[i] = 0
        start_ref[i] = begin
        qstart_ref[i] = qbegin
        begin = begin + far_count_ref[i]
        qbegin = qbegin + (count_ref[i] + GROUP - 1) // GROUP * GROUP
    keys_ref[...] = jnp.zeros(keys_ref.shape, keys_ref.dtype)
    vals_ref[...] = jnp.zeros(vals_ref.shape, vals_ref.dtype)

    def place(s, carry):
        for i in range(per):
            image = image_ref[(s * parts + other) * per + i]
            spot = start_ref[image]
            start_ref[image] = spot + 1
            put_block(keys_ref, vals_ref, spot, far_ref[s, i * BS : (i + 1) * BS, :])
            image_near = image_ref[(s * parts + mine) * per + i]
            seen = seen_ref[image_near]
            seen_ref[image_near] = seen + 1
            pos_ref[s * per + i] = qstart_ref[image_near] + seen

            @pl.when(seen >= count_ref[image_near] // WIDE * WIDE)
            def _():
                near = start_ref[image_near]
                start_ref[image_near] = near + 1
                put_block(keys_ref, vals_ref, near, got_ref[s, i * BS : (i + 1) * BS, :])

        return carry

    lax.fori_loop(0, sources, place, 0)

    def one_image(image, carry):
        tiles = (count_ref[image] + GROUP - 1) // GROUP
        count = far_count_ref[image]
        first = start_ref[image] - count
        qfirst = qstart_ref[image]

        def one_tile(t, carry):
            at = pl.ds(pl.multiple_of((qfirst + t * GROUP) * BS, BS), GROUP * BS)
            query = q_ref[at, :]

            def full(c, state):
                row = pl.ds(pl.multiple_of((first + c * WIDE) * BS, BS), WIDE * BS)
                return fold(state, score(query, keys_ref[row, :]), vals_ref[row, :])

            def rest(state):
                done = count // WIDE * WIDE
                row = pl.ds(pl.multiple_of((first + done) * BS, BS), WIDE * BS)
                spot = lax.broadcasted_iota(jnp.int32, (1, WIDE * BS), 1)
                scores = score(query, keys_ref[row, :])
                scores = jnp.where(spot < (count - done) * BS, scores, neg_large)
                return fold(state, scores, vals_ref[row, :])

            state = (best_ref[at, :][:, :1], accum_ref[at, :])
            state = lax.fori_loop(0, count // WIDE, full, state)
            best, accum = lax.cond(count % WIDE > 0, rest, lambda state: state, state)
            total = jnp.concatenate([accum[:, HD:], accum[:, :HD]], axis=1)
            o_ref[at, :] = accum / total
            return carry

        return lax.fori_loop(0, tiles, one_tile, carry)

    lax.fori_loop(0, images, one_image, 0)

    def emit(j, carry):
        half = BS // 2
        block = o_ref[pl.ds(pl.multiple_of(pos_ref[j] * BS, BS), BS), :].astype(jnp.bfloat16)
        out_ref[j] = jnp.concatenate([block[:half, HD:], block[half:, HD:]], axis=1)
        return carry

    lax.fori_loop(0, out_ref.shape[0], emit, 0)


def project_kernel(
    where_ref, image_ref, got_ref, w0_ref, w1_ref, w2_ref, w3_ref, gate_ref, res_ref, out_ref, mixed_ref
):
    groups = mixed_ref.shape[0]
    heads = mixed_ref.shape[2] // HD
    half = got_ref.shape[1]
    parts = got_ref.shape[0] // (groups * heads)
    for g in range(groups):
        for r in range(parts):
            pieces = [got_ref[(h * parts + r) * groups + g] for h in range(heads)]
            low = r * 2 * half
            mixed_ref[g, low : low + half, :] = jnp.concatenate(
                [piece[:, :HD] for piece in pieces], axis=1
            )
            mixed_ref[g, low + half : low + 2 * half, :] = jnp.concatenate(
                [piece[:, HD:] for piece in pieces], axis=1
            )
    me = where_ref[0]
    total = jnp.dot(mixed_ref[me], w0_ref[...], preferred_element_type=jnp.float32)
    for k, w_ref in ((1, w1_ref), (2, w2_ref), (3, w3_ref)):
        total += jnp.dot(mixed_ref[me ^ k], w_ref[...], preferred_element_type=jnp.float32)
    gating = gate_ref[pl.ds(image_ref[where_ref[1]], 1), :]
    out_ref[...] = (res_ref[...].astype(jnp.float32) + gating * total).astype(jnp.bfloat16)


def by_heads(
    queries, key_rows, values, text_keys, text_values, block_image, gate_image, residual, w_out
):
    tok_blk, ncols = queries.shape
    heads = ncols // HD
    nblk = lax.axis_size("blk")
    nhead = lax.axis_size("head")
    nblocks = block_image.shape[0]
    images = gate_image.shape[0]
    parts = nblk // heads
    blk = lax.axis_index("blk")
    head = lax.axis_index("head")
    smem = pl.BlockSpec(memory_space=pltpu.SMEM)
    vmem = pl.BlockSpec(memory_space=pltpu.VMEM)
    packed = tok_blk + tok_blk // 2
    local = nblocks // parts
    slots = round_up(local, GROUP) + GROUP * images
    groups = [[s * parts + y for s in range(heads)] for y in range(parts)]
    wide_groups = [[b * nhead + x for b in group for x in range(nhead)] for group in groups]
    text_rows = round_up(text_keys.shape[0], 16) + 256
    bf16 = jnp.bfloat16
    w1 = lax.ppermute(w_out, "head", [(i, i ^ 1) for i in range(nhead)])
    w2 = lax.ppermute(w_out, "head", [(i, i ^ 2) for i in range(nhead)])
    w3 = lax.ppermute(w2, "head", [(i, i ^ 1) for i in range(nhead)])
    send, text = pl.pallas_call(
        pack_kernel,
        out_shape=(
            jax.ShapeDtypeStruct((heads, packed, 2 * HD), bf16),
            jax.ShapeDtypeStruct((text_rows, 2 * HD), bf16),
        ),
        in_specs=[smem] + [vmem] * 5,
        out_specs=(vmem, vmem),
        name="pack",
    )((blk // parts).reshape(1), queries, key_rows, values, text_keys, text_values)
    got = lax.all_to_all(
        send, "blk", split_axis=0, concat_axis=0, tiled=True, axis_index_groups=groups
    )
    swap = [(i, i ^ 1) for i in range(nblk)]
    far = lax.ppermute(got[:, :tok_blk], "blk", swap)
    mine = (blk % parts).reshape(1)
    state_shape = (slots * BS, 2 * HD)
    state = pl.pallas_call(
        first_kernel,
        out_shape=(
            jax.ShapeDtypeStruct(state_shape, bf16),
            jax.ShapeDtypeStruct(state_shape, jnp.float32),
            jax.ShapeDtypeStruct(state_shape, jnp.float32),
        ),
        in_specs=[smem, smem, vmem, vmem],
        out_specs=(vmem, vmem, vmem),
        scratch_shapes=[pltpu.VMEM((local * BS, 2 * HD), bf16)] * 2
        + [pltpu.SMEM((images,), jnp.int32)] * 3,
        cost_estimate=pl.CostEstimate(
            flops=8 * HD * local * local * BS * BS,
            transcendentals=local * local * BS * BS,
            bytes_accessed=heads * packed * 4 * HD,
        ),
        name="attend_near",
    )(block_image, mine, got, text)
    key_slots = local + (WIDE - 1) * images + WIDE
    attended = pl.pallas_call(
        second_kernel,
        out_shape=jax.ShapeDtypeStruct((local, BS // 2, 2 * HD), bf16),
        in_specs=[smem, smem] + [vmem] * 5,
        out_specs=vmem,
        scratch_shapes=[pltpu.VMEM((key_slots * BS, 2 * HD), bf16)] * 2
        + [pltpu.VMEM(state_shape, jnp.float32)]
        + [pltpu.SMEM((images,), jnp.int32)] * 5
        + [pltpu.SMEM((local,), jnp.int32)],
        cost_estimate=pl.CostEstimate(
            flops=8 * HD * local * local * BS * BS,
            transcendentals=local * local * BS * BS,
            bytes_accessed=heads * packed * 4 * HD,
        ),
        name="attend_far",
    )(block_image, mine, got, far, *state)
    mixed = lax.all_to_all(
        attended,
        ("blk", "head"),
        split_axis=0,
        concat_axis=0,
        tiled=True,
        axis_index_groups=wide_groups,
    )
    return pl.pallas_call(
        project_kernel,
        out_shape=jax.ShapeDtypeStruct(residual.shape, bf16),
        in_specs=[smem, smem] + [vmem] * 7,
        out_specs=vmem,
        scratch_shapes=[pltpu.VMEM((nhead, BS, ncols), bf16)],
        name="project",
    )(
        jnp.stack([head, blk * nhead + head]),
        block_image,
        mixed,
        w_out,
        w1,
        w2,
        w3,
        gate_image,
        residual,
    )


def solution(mesh):
    placed = (
        P("blk", "head"),
        P("blk", "head"),
        P("blk", "head"),
        P(None, "head"),
        P(None, "head"),
        P(),
        P(),
        P(("blk", "head"), None),
        P("head", None),
    )
    nblk, nhead = mesh.shape["blk"], mesh.shape["head"]

    def step(queries, *others):
        heads = queries.shape[1] // HD
        fits = nhead == 4 and nblk % heads == 0 and nblk == 2 * heads
        fits = fits and queries.shape[0] == nhead * BS
        return (by_heads if fits else on_device)(queries, *others)

    return jax.shard_map(
        step, mesh=mesh, in_specs=placed, out_specs=P(("blk", "head"), None), check_vma=False
    )
```

profile of v0, /device:TPU:0, one launch (start us, length us, event | category | flops | bytes accessed | tf_op | source)
XLA Modules:
  0.0 81.2 jit_solution(4264635357646595157)
XLA Ops:
  0.0 0.0 copy-start.2
  0.0 2.6 %pack.1 = (bf16[4,768,128]{2,1,0:T(8,128)(2,1)}, bf16[576,128]{1,0:T(8,128)(2,1)}) custom-call(s32[1]{0:T(128)} %bitcast.3.head_ref, bf16[512,256]{1,0:T(8,128)(2,1)} %q_ref.1, bf16[512,256]{1,0:T(8,128)(2,1)} %k_ref.1, bf16[512,256]{1,0:T(8,128)(2,1)} %v_ref.1, bf16[308,256]{1,0:T(8,128)(2,1)} %tk_ref.1, bf16[308,256]{1,0:T(8,128)(2,1)} %tv_ref.1), custom_call_target="tpu_custom_call" | custom-call | tf_op jit(solution)/shard_map/pack/pallas_call | solution.py:364
  2.6 6.4 %all-to-all-start = ((bf16[4,768,128]{2,1,0:T(8,128)(2,1)}), bf16[4,768,128]{2,1,0:T(8,128)(2,1)S(1)}, u32[]{:S(2)}, u32[]{:S(2)}) async-start(bf16[4,768,128]{2,1,0:T(8,128)(2,1)} %get-tuple-element.10), calls=%async_computation | async-start | bytes 1572864 | tf_op jit(solution)/shard_map/all_to_all | solution.py:374
  8.9 0.0 copy-done.2
  8.9 1.5 %collective-permute-start.2 = (bf16[256,1536]{1,0:T(8,128)(2,1)S(1)}, bf16[256,1536]{1,0:T(8,128)(2,1)S(1)}, u32[]{:S(2)}, u32[]{:S(2)}) collective-permute-start(bf16[256,1536]{1,0:T(8,128)(2,1)S(1)} %copy-done.2), channel_id=1, source_target_pairs={{0,2},{1,3},{2,0},{3,1},{4,6},{5,7},{6,4},{7,5},{8,10},{9,11},{10,... | collective-permute-start | bytes 2359304 | tf_op jit(solution)/shard_map/ppermute | solution.py:362
  10.4 18.6 %all-to-all-done.got_ref = bf16[4,768,128]{2,1,0:T(8,128)(2,1)S(1)} async-done(((bf16[4,768,128]{2,1,0:T(8,128)(2,1)}), bf16[4,768,128]{2,1,0:T(8,128)(2,1)S(1)}, u32[]{:S(2)}, u32[]{:S(2)}) %all-to-all-start) | async-done | bytes 786464 | tf_op jit(solution)/shard_map/all_to_all | solution.py:374
  29.1 0.9 %slice.4 = bf16[4,512,128]{2,1,0:T(8,128)(2,1)} slice(bf16[4,768,128]{2,1,0:T(8,128)(2,1)S(1)} %all-to-all-done.got_ref), slice={[0:4], [0:512], [0:128]} | slice | bytes 1048576 | tf_op jit(solution)/shard_map/slice | solution.py:378
  30.0 1.5 %collective-permute-start = (bf16[4,512,128]{2,1,0:T(8,128)(2,1)}, bf16[4,512,128]{2,1,0:T(8,128)(2,1)}, u32[]{:S(2)}, u32[]{:S(2)}) collective-permute-start(bf16[4,512,128]{2,1,0:T(8,128)(2,1)} %slice.4), channel_id=1, source_target_pairs={{0,4},{4,0},{8,12},{12,8},{16,20},{20,16},{24,28},{28,24},{1,5},{5... | collective-permute-start | bytes 1572872 | tf_op jit(solution)/shard_map/ppermute | solution.py:378
  31.5 0.0 collective-permute-start.1
  31.5 0.0 collective-permute-done.2.w2_ref
  31.5 0.5 collective-permute-start.3
  32.0 0.0 copy-done
  32.0 11.9 %attend_near.1 = (bf16[2560,128]{1,0:T(8,128)(2,1)}, f32[2560,128]{1,0:T(8,128)}, f32[2560,128]{1,0:T(8,128)}) custom-call(s32[32]{0:T(128)} %image_ref.5, s32[1]{0:T(128)} %bitcast.2.where_ref, bf16[4,768,128]{2,1,0:T(8,128)(2,1)} %copy-done, bf16[576,128]{1,0:T(8,128)(2,1)} %get-tuple-element.11.text_ref), custom_call_target="tpu_custom_call" | custom-call | flops 2147483648 | bytes 786432 | tf_op jit(solution)/shard_map/attend_near/pallas_call | solution.py:381
  43.9 0.0 copy-done.3
  43.9 0.0 collective-permute-done.far_ref
  43.9 19.3 %attend_far.1 = bf16[16,64,128]{2,1,0:T(8,128)(2,1)} custom-call(s32[32]{0:T(128)} %image_ref.5, s32[1]{0:T(128)} %bitcast.2.where_ref, bf16[4,768,128]{2,1,0:T(8,128)(2,1)} %copy-done, bf16[4,512,128]{2,1,0:T(8,128)(2,1)} %collective-permute-done.far_ref, bf16[2560,128]{1,0:T(8,128)(2,1)} %get-tuple-element.12.q_ref, ...), custom_call_target="tpu_custom_call" | custom-call | flops 2147483648 | bytes 786432 | tf_op jit(solution)/shard_map/attend_far/pallas_call | solution.py:400
  63.2 3.8 %all-to-all-start.1 = ((bf16[16,64,128]{2,1,0:T(8,128)(2,1)}), bf16[16,64,128]{2,1,0:T(8,128)(2,1)S(1)}, u32[]{:S(2)}, u32[]{:S(2)}) async-start(bf16[16,64,128]{2,1,0:T(8,128)(2,1)} %attend_far.1), calls=%async_computation.1 | async-start | bytes 524288 | tf_op jit(solution)/shard_map/all_to_all | solution.py:416
  67.0 0.7 pad_add_fusion.where_ref
  67.6 0.0 collective-permute-done.1.w1_ref
  67.6 0.0 collective-permute-done.3.w3_ref
  67.6 9.3 %all-to-all-done.1.got_ref = bf16[16,64,128]{2,1,0:T(8,128)(2,1)S(1)} async-done(((bf16[16,64,128]{2,1,0:T(8,128)(2,1)}), bf16[16,64,128]{2,1,0:T(8,128)(2,1)S(1)}, u32[]{:S(2)}, u32[]{:S(2)}) %all-to-all-start.1) | async-done | bytes 262176 | tf_op jit(solution)/shard_map/all_to_all | solution.py:416
  77.0 0.0 copy-done.4
  77.0 0.7 copy-done.1
  77.7 3.5 %project.1 = bf16[128,1536]{1,0:T(8,128)(2,1)} custom-call(s32[2]{0:T(128)} %pad_add_fusion.where_ref, s32[32]{0:T(128)} %image_ref.5, bf16[16,64,128]{2,1,0:T(8,128)(2,1)} %copy-done.1, bf16[256,1536]{1,0:T(8,128)(2,1)} %w0_ref.1, bf16[256,1536]{1,0:T(8,128)(2,1)} %copy-done.4, bf16[256,1536]{1,0:T(8,128)(2,1)} %copy-done.3, ...), custom_call_target="tpu_custom_call" | custom-call | tf_op jit(solution)/shard_map/project/pallas_call | solution.py:424
  (4 shorter events, 0.0 us)
Async XLA Ops:
  0.0 8.9 %copy-start.2 = (bf16[256,1536]{1,0:T(8,128)(2,1)S(1)}, bf16[256,1536]{1,0:T(8,128)(2,1)}, u32[]{:S(2)}) copy-start(bf16[256,1536]{1,0:T(8,128)(2,1)} %w0_ref.1) | copy-start | bytes 2359300
  2.6 26.5 %all-to-all-start = ((bf16[4,768,128]{2,1,0:T(8,128)(2,1)}), bf16[4,768,128]{2,1,0:T(8,128)(2,1)S(1)}, u32[]{:S(2)}, u32[]{:S(2)}) async-start(bf16[4,768,128]{2,1,0:T(8,128)(2,1)} %get-tuple-element.10), calls=%async_computation | async-start | bytes 1572864 | tf_op jit(solution)/shard_map/all_to_all | solution.py:374
  8.9 22.5 %collective-permute-start.2 = (bf16[256,1536]{1,0:T(8,128)(2,1)S(1)}, bf16[256,1536]{1,0:T(8,128)(2,1)S(1)}, u32[]{:S(2)}, u32[]{:S(2)}) collective-permute-start(bf16[256,1536]{1,0:T(8,128)(2,1)S(1)} %copy-done.2), channel_id=1, source_target_pairs={{0,2},{1,3},{2,0},{3,1},{4,6},{5,7},{6,4},{7,5},{8,10},{9,11},{10,... | collective-permute-start | bytes 2359304 | tf_op jit(solution)/shard_map/ppermute | solution.py:362
  29.1 2.9 %copy-start = (bf16[4,768,128]{2,1,0:T(8,128)(2,1)}, bf16[4,768,128]{2,1,0:T(8,128)(2,1)S(1)}, u32[]{:S(2)}) copy-start(bf16[4,768,128]{2,1,0:T(8,128)(2,1)S(1)} %all-to-all-done.got_ref) | copy-start | bytes 2359300
  30.0 13.9 %collective-permute-start = (bf16[4,512,128]{2,1,0:T(8,128)(2,1)}, bf16[4,512,128]{2,1,0:T(8,128)(2,1)}, u32[]{:S(2)}, u32[]{:S(2)}) collective-permute-start(bf16[4,512,128]{2,1,0:T(8,128)(2,1)} %slice.4), channel_id=1, source_target_pairs={{0,4},{4,0},{8,12},{12,8},{16,20},{20,16},{24,28},{28,24},{1,5},{5... | collective-permute-start | bytes 1572872 | tf_op jit(solution)/shard_map/ppermute | solution.py:378
  31.5 36.1 %collective-permute-start.1 = (bf16[256,1536]{1,0:T(8,128)(2,1)S(1)}, bf16[256,1536]{1,0:T(8,128)(2,1)S(1)}, u32[]{:S(2)}, u32[]{:S(2)}) collective-permute-start(bf16[256,1536]{1,0:T(8,128)(2,1)S(1)} %copy-done.2), channel_id=1, source_target_pairs={{0,1},{1,0},{2,3},{3,2},{4,5},{5,4},{6,7},{7,6},{8,9},{9,8},{10,11... | collective-permute-start | bytes 2359304 | tf_op jit(solution)/shard_map/ppermute | solution.py:361
  31.5 12.4 %copy-start.3 = (bf16[256,1536]{1,0:T(8,128)(2,1)}, bf16[256,1536]{1,0:T(8,128)(2,1)S(1)}, u32[]{:S(2)}) copy-start(bf16[256,1536]{1,0:T(8,128)(2,1)S(1)} %collective-permute-done.2.w2_ref) | copy-start | bytes 2359300
  31.5 36.1 %collective-permute-start.3 = (bf16[256,1536]{1,0:T(8,128)(2,1)S(1)}, bf16[256,1536]{1,0:T(8,128)(2,1)}, u32[]{:S(2)}, u32[]{:S(2)}) collective-permute-start(bf16[256,1536]{1,0:T(8,128)(2,1)S(1)} %collective-permute-done.2.w2_ref), channel_id=1, source_target_pairs={{0,1},{1,0},{2,3},{3,2},{4,5},{5,4},{6,7},{7,6},{8,9},{9,8},{10,11... | collective-permute-start | bytes 2359304 | tf_op jit(solution)/shard_map/ppermute | solution.py:363
  63.2 13.8 %all-to-all-start.1 = ((bf16[16,64,128]{2,1,0:T(8,128)(2,1)}), bf16[16,64,128]{2,1,0:T(8,128)(2,1)S(1)}, u32[]{:S(2)}, u32[]{:S(2)}) async-start(bf16[16,64,128]{2,1,0:T(8,128)(2,1)} %attend_far.1), calls=%async_computation.1 | async-start | bytes 524288 | tf_op jit(solution)/shard_map/all_to_all | solution.py:416
  67.6 9.3 %copy-start.4 = (bf16[256,1536]{1,0:T(8,128)(2,1)}, bf16[256,1536]{1,0:T(8,128)(2,1)S(1)}, u32[]{:S(2)}) copy-start(bf16[256,1536]{1,0:T(8,128)(2,1)S(1)} %collective-permute-done.1.w1_ref) | copy-start | bytes 2359300
  77.0 0.7 copy-start.1
where the time goes:
time: 81.5 us; the launch traced here: 81.2 us
  Pallas kernels  37.2 us (46%)
  waiting for transfers between devices  27.9 us (34%)
  starting transfers between devices  13.7 us (17%)
  local copies, waits for them, and re-layouts  1.64 us (2%)
    pallas_call x1, Pallas kernels, by_heads(): pl.pallas_call(second_kernel, out_shape=jax.ShapeDtypeStruct((local, BS /...  19.3 us
    all_to_all x1, waiting for transfers between devices, by_heads(): lax.all_to_all(send, 'blk', split_axis=0, concat_axis=0, tiled=True, axis...  18.6 us
    pallas_call x1, Pallas kernels, by_heads(): pl.pallas_call(first_kernel, out_shape=(jax.ShapeDtypeStruct(state_shape,...  11.9 us
    all_to_all x1, waiting for transfers between devices, by_heads(): lax.all_to_all(attended, ('blk', 'head'), split_axis=0, concat_axis=0, ti...  9.33 us
    all_to_all x1, starting transfers between devices, by_heads(): lax.all_to_all(send, 'blk', split_axis=0, concat_axis=0, tiled=True, axis...  6.35 us
    all_to_all x1, starting transfers between devices, by_heads(): lax.all_to_all(attended, ('blk', 'head'), split_axis=0, concat_axis=0, ti...  3.78 us
    pallas_call x1, Pallas kernels, by_heads(): pl.pallas_call(project_kernel, out_shape=jax.ShapeDtypeStruct(residual.sh...  3.47 us
    pallas_call x1, Pallas kernels, by_heads(): pl.pallas_call(pack_kernel, out_shape=(jax.ShapeDtypeStruct((heads, packe...  2.59 us
  transfers between devices with their start and end apart: 6, of which 2 were waited for; matrix products, arithmetic and copies ran while one was open for 2% of the time, Pallas kernels for 38%

commit v1 on v0

--- a/solution.py
+++ b/solution.py
@@ -10,7 +10,7 @@
 HD = 64
 TEXT = 154
 BS = 128
-GROUP = 2
+GROUP = 4
 WIDE = 8
 
 

time: 81.5 us -> 78.6 us (0.964); the launches traced: 81.2 us -> 79.7 us
  Pallas kernels: 37.2 us -> 35 us
  waiting for transfers between devices: 27.9 us -> 29 us
    pallas_call x1, Pallas kernels: 11.9 us -> 10.1 us  [by_heads(): pl.pallas_call(first_kernel, out_shape=(jax.ShapeDtypeStruct(state_shape,...]
    ppermute x1, waiting for transfers between devices: 0.01 us -> 1.09 us  [by_heads(): far = lax.ppermute(got[:, :tok_blk], 'blk', swap)]
  transfers between devices with their start and end apart: 6 -> 6, of which waited for: 2 -> 3; matrix products, arithmetic and copies ran while one was open for 2% -> 2% of each run, Pallas kernels for 38% -> 36%
where the time goes in v1:
time: 78.6 us; the launch traced here: 79.7 us
  Pallas kernels  35 us (45%)
  waiting for transfers between devices  29 us (37%)
  starting transfers between devices  13.4 us (17%)
  local copies, waits for them, and re-layouts  1.61 us (2%)
    pallas_call x1, Pallas kernels, by_heads(): pl.pallas_call(second_kernel, out_shape=jax.ShapeDtypeStruct((local, BS /...  18.8 us
    all_to_all x1, waiting for transfers between devices, by_heads(): lax.all_to_all(send, 'blk', split_axis=0, concat_axis=0, tiled=True, axis...  18.6 us
    pallas_call x1, Pallas kernels, by_heads(): pl.pallas_call(first_kernel, out_shape=(jax.ShapeDtypeStruct(state_shape,...  10.1 us
    all_to_all x1, waiting for transfers between devices, by_heads(): lax.all_to_all(attended, ('blk', 'head'), split_axis=0, concat_axis=0, ti...  9.29 us
    all_to_all x1, starting transfers between devices, by_heads(): lax.all_to_all(send, 'blk', split_axis=0, concat_axis=0, tiled=True, axis...  6.35 us
    all_to_all x1, starting transfers between devices, by_heads(): lax.all_to_all(attended, ('blk', 'head'), split_axis=0, concat_axis=0, ti...  3.53 us
    pallas_call x1, Pallas kernels, by_heads(): pl.pallas_call(project_kernel, out_shape=jax.ShapeDtypeStruct(residual.sh...  3.47 us
    pallas_call x1, Pallas kernels, by_heads(): pl.pallas_call(pack_kernel, out_shape=(jax.ShapeDtypeStruct((heads, packe...  2.59 us
  transfers between devices with their start and end apart: 6, of which 3 were waited for; matrix products, arithmetic and copies ran while one was open for 2% of the time, Pallas kernels for 36%

profile of v1, /device:TPU:0, one launch (start us, length us, event | category | flops | bytes accessed | tf_op | source)
XLA Modules:
  0.0 79.7 jit_solution(17924486875782195732)
XLA Ops:
  0.0 0.0 copy-start.2
  0.0 2.6 %pack.1 = (bf16[4,768,128]{2,1,0:T(8,128)(2,1)}, bf16[576,128]{1,0:T(8,128)(2,1)}) custom-call(s32[1]{0:T(128)} %bitcast.3.head_ref, bf16[512,256]{1,0:T(8,128)(2,1)} %q_ref.1, bf16[512,256]{1,0:T(8,128)(2,1)} %k_ref.1, bf16[512,256]{1,0:T(8,128)(2,1)} %v_ref.1, bf16[308,256]{1,0:T(8,128)(2,1)} %tk_ref.1, bf16[308,256]{1,0:T(8,128)(2,1)} %tv_ref.1), custom_call_target="tpu_custom_call" | custom-call | tf_op jit(solution)/shard_map/pack/pallas_call | solution.py:364
  2.6 6.4 %all-to-all-start = ((bf16[4,768,128]{2,1,0:T(8,128)(2,1)}), bf16[4,768,128]{2,1,0:T(8,128)(2,1)S(1)}, u32[]{:S(2)}, u32[]{:S(2)}) async-start(bf16[4,768,128]{2,1,0:T(8,128)(2,1)} %get-tuple-element.10), calls=%async_computation | async-start | bytes 1572864 | tf_op jit(solution)/shard_map/all_to_all | solution.py:374
  8.9 0.0 copy-done.2
  8.9 1.5 %collective-permute-start.2 = (bf16[256,1536]{1,0:T(8,128)(2,1)S(1)}, bf16[256,1536]{1,0:T(8,128)(2,1)S(1)}, u32[]{:S(2)}, u32[]{:S(2)}) collective-permute-start(bf16[256,1536]{1,0:T(8,128)(2,1)S(1)} %copy-done.2), channel_id=1, source_target_pairs={{0,2},{1,3},{2,0},{3,1},{4,6},{5,7},{6,4},{7,5},{8,10},{9,11},{10,... | collective-permute-start | bytes 2359304 | tf_op jit(solution)/shard_map/ppermute | solution.py:362
  10.4 18.6 %all-to-all-done.got_ref = bf16[4,768,128]{2,1,0:T(8,128)(2,1)S(1)} async-done(((bf16[4,768,128]{2,1,0:T(8,128)(2,1)}), bf16[4,768,128]{2,1,0:T(8,128)(2,1)S(1)}, u32[]{:S(2)}, u32[]{:S(2)}) %all-to-all-start) | async-done | bytes 786464 | tf_op jit(solution)/shard_map/all_to_all | solution.py:374
  29.1 0.9 %slice.4 = bf16[4,512,128]{2,1,0:T(8,128)(2,1)} slice(bf16[4,768,128]{2,1,0:T(8,128)(2,1)S(1)} %all-to-all-done.got_ref), slice={[0:4], [0:512], [0:128]} | slice | bytes 1048576 | tf_op jit(solution)/shard_map/slice | solution.py:378
  29.9 1.5 %collective-permute-start = (bf16[4,512,128]{2,1,0:T(8,128)(2,1)}, bf16[4,512,128]{2,1,0:T(8,128)(2,1)}, u32[]{:S(2)}, u32[]{:S(2)}) collective-permute-start(bf16[4,512,128]{2,1,0:T(8,128)(2,1)} %slice.4), channel_id=1, source_target_pairs={{0,4},{4,0},{8,12},{12,8},{16,20},{20,16},{24,28},{28,24},{1,5},{5... | collective-permute-start | bytes 1572872 | tf_op jit(solution)/shard_map/ppermute | solution.py:378
  31.4 0.0 collective-permute-start.1
  31.5 0.0 collective-permute-done.2.w2_ref
  31.5 0.5 collective-permute-start.3
  32.0 0.0 copy-done
  32.0 10.1 %attend_near.1 = (bf16[3072,128]{1,0:T(8,128)(2,1)}, f32[3072,128]{1,0:T(8,128)}, f32[3072,128]{1,0:T(8,128)}) custom-call(s32[32]{0:T(128)} %image_ref.5, s32[1]{0:T(128)} %bitcast.2.where_ref, bf16[4,768,128]{2,1,0:T(8,128)(2,1)} %copy-done, bf16[576,128]{1,0:T(8,128)(2,1)} %get-tuple-element.11.text_ref), custom_call_target="tpu_custom_call" | custom-call | flops 2147483648 | bytes 786432 | tf_op jit(solution)/shard_map/attend_near/pallas_call | solution.py:381
  42.1 0.0 copy-done.3
  42.1 1.1 %collective-permute-done.far_ref = bf16[4,512,128]{2,1,0:T(8,128)(2,1)} collective-permute-done((bf16[4,512,128]{2,1,0:T(8,128)(2,1)}, bf16[4,512,128]{2,1,0:T(8,128)(2,1)}, u32[]{:S(2)}, u32[]{:S(2)}) %collective-permute-start) | collective-permute-done | bytes 524320 | tf_op jit(solution)/shard_map/ppermute | solution.py:378
  43.2 18.8 %attend_far.1 = bf16[16,64,128]{2,1,0:T(8,128)(2,1)} custom-call(s32[32]{0:T(128)} %image_ref.5, s32[1]{0:T(128)} %bitcast.2.where_ref, bf16[4,768,128]{2,1,0:T(8,128)(2,1)} %copy-done, bf16[4,512,128]{2,1,0:T(8,128)(2,1)} %collective-permute-done.far_ref, bf16[3072,128]{1,0:T(8,128)(2,1)} %get-tuple-element.12.q_ref, ...), custom_call_target="tpu_custom_call" | custom-call | flops 2147483648 | bytes 786432 | tf_op jit(solution)/shard_map/attend_far/pallas_call | solution.py:400
  62.0 3.5 %all-to-all-start.1 = ((bf16[16,64,128]{2,1,0:T(8,128)(2,1)}), bf16[16,64,128]{2,1,0:T(8,128)(2,1)S(1)}, u32[]{:S(2)}, u32[]{:S(2)}) async-start(bf16[16,64,128]{2,1,0:T(8,128)(2,1)} %attend_far.1), calls=%async_computation.1 | async-start | bytes 524288 | tf_op jit(solution)/shard_map/all_to_all | solution.py:416
  65.5 0.7 pad_add_fusion.where_ref
  66.2 0.0 collective-permute-done.1.w1_ref
  66.2 0.0 collective-permute-done.3.w3_ref
  66.2 9.3 %all-to-all-done.1.got_ref = bf16[16,64,128]{2,1,0:T(8,128)(2,1)S(1)} async-done(((bf16[16,64,128]{2,1,0:T(8,128)(2,1)}), bf16[16,64,128]{2,1,0:T(8,128)(2,1)S(1)}, u32[]{:S(2)}, u32[]{:S(2)}) %all-to-all-start.1) | async-done | bytes 262176 | tf_op jit(solution)/shard_map/all_to_all | solution.py:416
  75.5 0.0 copy-done.4
  75.5 0.7 copy-done.1
  76.2 3.5 %project.1 = bf16[128,1536]{1,0:T(8,128)(2,1)} custom-call(s32[2]{0:T(128)} %pad_add_fusion.where_ref, s32[32]{0:T(128)} %image_ref.5, bf16[16,64,128]{2,1,0:T(8,128)(2,1)} %copy-done.1, bf16[256,1536]{1,0:T(8,128)(2,1)} %w0_ref.1, bf16[256,1536]{1,0:T(8,128)(2,1)} %copy-done.4, bf16[256,1536]{1,0:T(8,128)(2,1)} %copy-done.3, ...), custom_call_target="tpu_custom_call" | custom-call | tf_op jit(solution)/shard_map/project/pallas_call | solution.py:424
  (4 shorter events, 0.0 us)
Async XLA Ops:
  0.0 8.9 %copy-start.2 = (bf16[256,1536]{1,0:T(8,128)(2,1)S(1)}, bf16[256,1536]{1,0:T(8,128)(2,1)}, u32[]{:S(2)}) copy-start(bf16[256,1536]{1,0:T(8,128)(2,1)} %w0_ref.1) | copy-start | bytes 2359300
  2.6 26.5 %all-to-all-start = ((bf16[4,768,128]{2,1,0:T(8,128)(2,1)}), bf16[4,768,128]{2,1,0:T(8,128)(2,1)S(1)}, u32[]{:S(2)}, u32[]{:S(2)}) async-start(bf16[4,768,128]{2,1,0:T(8,128)(2,1)} %get-tuple-element.10), calls=%async_computation | async-start | bytes 1572864 | tf_op jit(solution)/shard_map/all_to_all | solution.py:374
  8.9 22.5 %collective-permute-start.2 = (bf16[256,1536]{1,0:T(8,128)(2,1)S(1)}, bf16[256,1536]{1,0:T(8,128)(2,1)S(1)}, u32[]{:S(2)}, u32[]{:S(2)}) collective-permute-start(bf16[256,1536]{1,0:T(8,128)(2,1)S(1)} %copy-done.2), channel_id=1, source_target_pairs={{0,2},{1,3},{2,0},{3,1},{4,6},{5,7},{6,4},{7,5},{8,10},{9,11},{10,... | collective-permute-start | bytes 2359304 | tf_op jit(solution)/shard_map/ppermute | solution.py:362
  29.1 2.9 %copy-start = (bf16[4,768,128]{2,1,0:T(8,128)(2,1)}, bf16[4,768,128]{2,1,0:T(8,128)(2,1)S(1)}, u32[]{:S(2)}) copy-start(bf16[4,768,128]{2,1,0:T(8,128)(2,1)S(1)} %all-to-all-done.got_ref) | copy-start | bytes 2359300
  29.9 13.3 %collective-permute-start = (bf16[4,512,128]{2,1,0:T(8,128)(2,1)}, bf16[4,512,128]{2,1,0:T(8,128)(2,1)}, u32[]{:S(2)}, u32[]{:S(2)}) collective-permute-start(bf16[4,512,128]{2,1,0:T(8,128)(2,1)} %slice.4), channel_id=1, source_target_pairs={{0,4},{4,0},{8,12},{12,8},{16,20},{20,16},{24,28},{28,24},{1,5},{5... | collective-permute-start | bytes 1572872 | tf_op jit(solution)/shard_map/ppermute | solution.py:378
  31.4 34.7 %collective-permute-start.1 = (bf16[256,1536]{1,0:T(8,128)(2,1)S(1)}, bf16[256,1536]{1,0:T(8,128)(2,1)S(1)}, u32[]{:S(2)}, u32[]{:S(2)}) collective-permute-start(bf16[256,1536]{1,0:T(8,128)(2,1)S(1)} %copy-done.2), channel_id=1, source_target_pairs={{0,1},{1,0},{2,3},{3,2},{4,5},{5,4},{6,7},{7,6},{8,9},{9,8},{10,11... | collective-permute-start | bytes 2359304 | tf_op jit(solution)/shard_map/ppermute | solution.py:361
  31.5 10.6 %copy-start.3 = (bf16[256,1536]{1,0:T(8,128)(2,1)}, bf16[256,1536]{1,0:T(8,128)(2,1)S(1)}, u32[]{:S(2)}) copy-start(bf16[256,1536]{1,0:T(8,128)(2,1)S(1)} %collective-permute-done.2.w2_ref) | copy-start | bytes 2359300
  31.5 34.7 %collective-permute-start.3 = (bf16[256,1536]{1,0:T(8,128)(2,1)S(1)}, bf16[256,1536]{1,0:T(8,128)(2,1)}, u32[]{:S(2)}, u32[]{:S(2)}) collective-permute-start(bf16[256,1536]{1,0:T(8,128)(2,1)S(1)} %collective-permute-done.2.w2_ref), channel_id=1, source_target_pairs={{0,1},{1,0},{2,3},{3,2},{4,5},{5,4},{6,7},{7,6},{8,9},{9,8},{10,11... | collective-permute-start | bytes 2359304 | tf_op jit(solution)/shard_map/ppermute | solution.py:363
  62.0 13.5 %all-to-all-start.1 = ((bf16[16,64,128]{2,1,0:T(8,128)(2,1)}), bf16[16,64,128]{2,1,0:T(8,128)(2,1)S(1)}, u32[]{:S(2)}, u32[]{:S(2)}) async-start(bf16[16,64,128]{2,1,0:T(8,128)(2,1)} %attend_far.1), calls=%async_computation.1 | async-start | bytes 524288 | tf_op jit(solution)/shard_map/all_to_all | solution.py:416
  66.2 9.3 %copy-start.4 = (bf16[256,1536]{1,0:T(8,128)(2,1)}, bf16[256,1536]{1,0:T(8,128)(2,1)S(1)}, u32[]{:S(2)}) copy-start(bf16[256,1536]{1,0:T(8,128)(2,1)S(1)} %collective-permute-done.1.w1_ref) | copy-start | bytes 2359300
  75.5 0.7 copy-start.1
